TPU v7x, 512 devices: a whole 4x8x8 slice. The times are simulated.
512 devices in a mesh: fsdp: 64 (over y_lo, z, core), tp: 8 (over x, y_hi).
Axes of the slice: x: 4, y: 8 (y_hi: 2, y_lo: 4; y = y_hi * 4 + y_lo), z: 8, core: 2. Of those that a mesh axis runs over, the one named last changes fastest.
Arguments:
- images: bfloat16 [64, 256, 6144], P('fsdp', None, 'tp'), may hold values from -6 to 6
- keep_index: int32 [64, 64], P('fsdp'), may hold values from 0 to 255, as said below
- teacher_weight: float32 [6144, 3072], P('fsdp', 'tp'), may hold values from -0.078125 to 0.078125
- student_weight: float32 [6144, 3072], P('fsdp', 'tp'), may hold values from -0.078125 to 0.078125
Outputs:
- teacher_next: float32 [6144, 3072], P('fsdp', 'tp')
- student_grad: float32 [6144, 3072], P('fsdp', 'tp')
Inputs may be any that keep to these rules, and one draw needn't show every extreme that they name: `keep_index`: each image's 64 indices are distinct and increasing.
All inputs are finite; a program needn't handle non-finite values.
Results may differ from a plain program's by a relative error of at most 0.0048.
Values may be sent and summed in bfloat16 or wider, within the bound.
No kernel may reach another device: no remote copies, remote signals or barrier semaphores. Data moves between devices by JAX's collectives and lax.ppermute only.
A program may use at most 64 MiB of HBM per device.

v0:
```python
import math
import jax
import jax.numpy as jnp
from jax import lax
from jax.sharding import PartitionSpec as P

D = 6144


def layer_norm(values):
    floats = values.astype(jnp.float32)
    centre = jnp.mean(floats, axis=-1, keepdims=True)
    centred = floats - centre
    spread = jnp.mean(centred * centred, axis=-1, keepdims=True)
    return (centred * lax.rsqrt(spread + 1e-06)).astype(jnp.bfloat16)


def pick_rows(table, index):
    return jax.vmap(lambda block, rows: block[rows])(table, index)


def row_product(features, piece):
    return jnp.dot(features, piece, preferred_element_type=jnp.float32)


def shards(images, keep_index, teacher_weight, student_weight):
    img_count = images.shape[0]
    patch_count = images.shape[1]
    keep_count = keep_index.shape[1]
    columns_dev = teacher_weight.shape[1]
    teacher_next = 0.999 * teacher_weight + (1.0 - 0.999) * student_weight
    teacher_panel = teacher_next.astype(jnp.bfloat16)
    student_panel = student_weight.astype(jnp.bfloat16)
    whole = lax.all_gather(images, "tp", axis=2, tiled=True)
    normed = layer_norm(whole)
    flat_all = normed.reshape(img_count * patch_count, D)
    picked = pick_rows(normed, keep_index).reshape(img_count * keep_count, D)
    teacher_out = row_product(flat_all, lax.all_gather(teacher_panel, "fsdp", axis=0, tiled=True))
    student_out = row_product(picked, lax.all_gather(student_panel, "fsdp", axis=0, tiled=True))
    teacher_out = teacher_out.reshape(img_count, patch_count, columns_dev)
    centre = jnp.mean(teacher_out, axis=1, keepdims=True)
    centred_out = teacher_out - centre
    spread = jnp.mean(centred_out * centred_out, axis=1, keepdims=True)
    target = centred_out * lax.rsqrt(spread + 1e-05)
    target_kept = pick_rows(target, keep_index).reshape(img_count * keep_count, columns_dev)
    total_kept = img_count * keep_count * lax.axis_size("fsdp")
    error = ((student_out - target_kept) * (1.0 / math.sqrt(total_kept))).astype(jnp.bfloat16)
    owned = lax.all_to_all(picked, "fsdp", split_axis=1, concat_axis=0, tiled=True)
    student_grad = lax.dot_general(
        owned,
        lax.all_gather(error, "fsdp", axis=0, tiled=True),
        (((0,), (0,)), ((), ())),
        preferred_element_type=jnp.float32,
    )
    return (teacher_next, student_grad)


def solution(mesh):
    placed = (P("fsdp", None, "tp"), P("fsdp", None), P("fsdp", "tp"), P("fsdp", "tp"))
    return jax.shard_map(
        shards,
        mesh=mesh,
        in_specs=placed,
        out_specs=(P("fsdp", "tp"), P("fsdp", "tp")),
        check_vma=False,
    )
```

profile of v0, /device:TPU:1, one launch (start us, length us, event | category | flops | bytes accessed | tf_op | source)
XLA Modules:
  0.0 498.9 jit_solution(11816537188644948361)
XLA Ops:
  7.2 0.0 all-gather.5.cloned.1.call-start
  7.2 0.7 all-gather.5.cloned.1.call-update
  7.9 0.0 all-gather.9.cloned.1.call-start
  7.9 1.8 fusion.9
  9.7 0.0 all-gather.9.cloned.1.call-update
  9.7 0.0 all-gather.7.cloned.1.call-start
  9.8 0.7 all-gather.7.cloned.1.call-update
  10.5 0.0 all-gather.11.cloned.1.call-start
  10.5 0.7 fusion.8
  11.2 97.9 %all-gather.5.cloned.1.call-done = bf16[1,256,6144]{2,1,0:T(8,128)(2,1)} async-done(((bf16[1,256,768]{2,1,0:T(8,128)(2,1)}), bf16[1,256,6144]{2,1,0:T(8,128)(2,1)}) %all-gather.5.cloned.1.call-update) | async-done | bytes 3145744 | tf_op jit(solution)/shard_map/all_gather | solution.py:34
  109.1 0.0 copy-start
  109.1 2.5 convert_reduce_fusion
  111.7 0.3 copy-done
  111.9 1.0 fusion.2
  112.9 1.2 fusion.3
  114.1 3.8 gather_fusion
  117.9 114.0 %all-gather.9.cloned.1.call-done = bf16[6144,384]{1,0:T(8,128)(2,1)} async-done(((bf16[96,384]{1,0:T(8,128)(2,1)}), bf16[6144,384]{1,0:T(8,128)(2,1)}) %all-gather.9.cloned.1.call-update) | async-done | bytes 4718608 | tf_op jit(solution)/shard_map/all_gather | solution.py:38
  231.9 4.3 fusion.10
  236.2 0.0 copy-start.1
  236.2 0.1 multiply_reduce_fusion
  236.3 0.8 gather_fusion.1
  237.1 116.3 %all-gather.7.cloned.1.call-done = bf16[6144,384]{1,0:T(8,128)(2,1)} async-done(((bf16[96,384]{1,0:T(8,128)(2,1)}), bf16[6144,384]{1,0:T(8,128)(2,1)}) %all-gather.7.cloned.1.call-update) | async-done | bytes 4718608 | tf_op jit(solution)/shard_map/all_gather | solution.py:39
  353.4 4.0 fusion.7
  357.4 0.0 all-gather.11.cloned.1.call-update
  357.4 0.0 copy-done.1
  357.4 1.0 all_to_all.14
  358.5 0.7 copy.6
  359.2 36.8 %all_to_all.19 = bf16[64,64,96]{2,0,1:T(8,128)(2,1)S(1)} all-to-all(bf16[64,64,96]{2,0,1:T(8,128)(2,1)S(1)} %copy.6), channel_id=1, replica_groups=mesh['fsdp'=64,'tp'=8] {'fsdp'}, dimensions={1} | all-to-all | bytes 1572864 | tf_op jit(solution)/shard_map/all_to_all | solution.py:48
  396.0 93.2 %all-gather.11.cloned.1.call-done = bf16[4096,384]{1,0:T(8,128)(2,1)} async-done(((bf16[64,384]{1,0:T(8,128)(2,1)}), bf16[4096,384]{1,0:T(8,128)(2,1)}) %all-gather.11.cloned.1.call-update) | async-done | bytes 3145744 | tf_op jit(solution)/shard_map/all_gather | solution.py:51
  489.2 3.3 fusion.11
  (7 shorter events, 0.1 us)
Async XLA Ops:
  7.2 101.9 %all-gather.5.cloned.1.call-start = ((), (), s32[]{:S(2)}) async-start(), calls=%async_computation.1 | async-start | bytes 3538944 | tf_op jit(solution)/shard_map/all_gather | solution.py:34
  7.9 224.0 %all-gather.9.cloned.1.call-start = ((), (), s32[]{:S(2)}) async-start(), calls=%async_computation.3 | async-start | bytes 4792320 | tf_op jit(solution)/shard_map/all_gather | solution.py:38
  9.7 343.6 %all-gather.7.cloned.1.call-start = ((), (), s32[]{:S(2)}) async-start(), calls=%async_computation.2 | async-start | bytes 4792320 | tf_op jit(solution)/shard_map/all_gather | solution.py:39
  10.5 478.7 %all-gather.11.cloned.1.call-start = ((), (), s32[]{:S(2)}) async-start(), calls=%async_computation.4 | async-start | bytes 3194880 | tf_op jit(solution)/shard_map/all_gather | solution.py:51
  109.1 2.8 copy-start
  236.2 121.3 %copy-start.1 = (bf16[64,6144]{1,0:T(8,128)(2,1)S(1)}, bf16[64,6144]{1,0:T(8,128)(2,1)}, u32[]{:S(2)}) copy-start(bf16[64,6144]{1,0:T(8,128)(2,1)} %gather_fusion) | copy-start | bytes 2359300
Sparse Core Ops, SparseCore 0:
  11.1 97.9 all-gather.4
  111.8 120.0 all-gather.8
  234.0 119.2 all-gather.6
  357.5 131.5 all-gather.10
where the time goes:
time: 499 us
  waiting for transfers between devices  423 us (85%)
  blocking collectives  36.8 us (7%)
  between operations  13.8 us (3%)
  matrix products  11.5 us (2%)
  other arithmetic  7.33 us (1%)
  local copies, waits for them, and re-layouts  6.58 us (1%)
    all_gather x1, waiting for transfers between devices, shards(): lax.all_gather(student_panel, 'fsdp', axis=0, tiled=True)  116 us
    all_gather x1, waiting for transfers between devices, shards(): lax.all_gather(teacher_panel, 'fsdp', axis=0, tiled=True)  114 us
    all_gather x1, waiting for transfers between devices, shards(): whole = lax.all_gather(images, 'tp', axis=2, tiled=True)  97.9 us
    all_gather x1, waiting for transfers between devices, shards(): lax.all_gather(error, 'fsdp', axis=0, tiled=True)  93.2 us
    all_to_all x1, blocking collectives, shards(): lax.all_to_all(picked, 'fsdp', split_axis=1, concat_axis=0, tiled=True)  36.8 us
  transfers between devices with their start and end apart: 4, of which 4 were waited for; matrix products, arithmetic and copies ran while one was open for 3% of the time, Pallas kernels for 0%

commit v1 on v0

--- a/solution.py
+++ b/solution.py
@@ -45,7 +45,10 @@
     target_kept = pick_rows(target, keep_index).reshape(img_count * keep_count, columns_dev)
     total_kept = img_count * keep_count * lax.axis_size("fsdp")
     error = ((student_out - target_kept) * (1.0 / math.sqrt(total_kept))).astype(jnp.bfloat16)
-    owned = lax.all_to_all(picked, "fsdp", split_axis=1, concat_axis=0, tiled=True)
+    owned = jnp.concatenate(
+        lax.all_to_all(jnp.stack(jnp.split(picked, lax.axis_size("fsdp"), axis=1)), "fsdp", 0, 0),
+        axis=0,
+    )
     student_grad = lax.dot_general(
         owned,
         lax.all_gather(error, "fsdp", axis=0, tiled=True),

time: 499 us -> 507 us (1.016); the launches traced: 499 us -> 500 us
  local copies, waits for them, and re-layouts: 6.58 us -> 94 us
  waiting for transfers between devices: 423 us -> 336 us
    unnamed x4 -> x65, local copies, waits for them, and re-layouts: 0.29 us -> 88.1 us
    all_gather x1, waiting for transfers between devices: 114 us -> 53.9 us  [shards(): lax.all_gather(teacher_panel, 'fsdp', axis=0, tiled=True)]
    all_gather x1, waiting for transfers between devices: 93.2 us -> 66.3 us  [shards(): lax.all_gather(error, 'fsdp', axis=0, tiled=True)]
  transfers between devices with their start and end apart: 4 -> 4, of which waited for: 4 -> 4; matrix products, arithmetic and copies ran while one was open for 3% -> 21% of each run, Pallas kernels for 0% -> 0%
where the time goes in v1:
time: 507 us; the launch traced here: 500 us
  waiting for transfers between devices  336 us (66%)
  local copies, waits for them, and re-layouts  94 us (19%)
  blocking collectives  37.4 us (7%)
  between operations  13.8 us (3%)
  matrix products  11.5 us (2%)
  other arithmetic  7.34 us (1%)
    all_gather x1, waiting for transfers between devices, shards(): lax.all_gather(student_panel, 'fsdp', axis=0, tiled=True)  117 us
    all_gather x1, waiting for transfers between devices, shards(): whole = lax.all_gather(images, 'tp', axis=2, tiled=True)  97.9 us
    unnamed x65, local copies, waits for them, and re-layouts  88.1 us
    all_gather x1, waiting for transfers between devices, shards(): lax.all_gather(error, 'fsdp', axis=0, tiled=True)  66.3 us
    all_gather x1, waiting for transfers between devices, shards(): lax.all_gather(teacher_panel, 'fsdp', axis=0, tiled=True)  53.9 us
    all_to_all x1, blocking collectives, shards(): lax.all_to_all(jnp.stack(jnp.split(picked, lax.axis_size('fsdp'), axis=1)...  37.4 us
  transfers between devices with their start and end apart: 4, of which 4 were waited for; matrix products, arithmetic and copies ran while one was open for 21% of the time, Pallas kernels for 0%

profile of v1, /device:TPU:1, one launch (start us, length us, event | category | flops | bytes accessed | tf_op | source)
XLA Modules:
  0.0 500.4 jit_solution(13496221525428990058)
XLA Ops:
  7.9 1.8 fusion.9
  11.2 97.9 %all-gather.5.cloned.1.call-done = bf16[1,256,6144]{2,1,0:T(8,128)(2,1)} async-done(((bf16[1,256,768]{2,1,0:T(8,128)(2,1)}), bf16[1,256,6144]{2,1,0:T(8,128)(2,1)}) %all-gather.5.cloned.1.call-update) | async-done | bytes 3145744 | tf_op jit(solution)/shard_map/all_gather | solution.py:34
  109.1 2.5 convert_reduce_fusion
  114.1 3.8 gather_fusion
  119.2 1.4 constant_dynamic-update-slice_fusion.62
  120.7 1.4 constant_dynamic-update-slice_fusion.61
  122.1 1.4 constant_dynamic-update-slice_fusion.60
  124.8 1.4 constant_dynamic-update-slice_fusion.58
  126.3 1.4 constant_dynamic-update-slice_fusion.57
  130.4 1.4 constant_dynamic-update-slice_fusion.54
  131.8 1.4 constant_dynamic-update-slice_fusion.53
  136.0 1.4 constant_dynamic-update-slice_fusion.50
  137.4 1.4 constant_dynamic-update-slice_fusion.49
  138.8 1.4 constant_dynamic-update-slice_fusion.48
  141.6 1.4 constant_dynamic-update-slice_fusion.46
  143.0 1.4 constant_dynamic-update-slice_fusion.45
  147.1 1.4 constant_dynamic-update-slice_fusion.42
  148.6 1.4 constant_dynamic-update-slice_fusion.41
  152.7 1.4 constant_dynamic-update-slice_fusion.38
  154.1 1.4 constant_dynamic-update-slice_fusion.37
  158.3 1.4 constant_dynamic-update-slice_fusion.34
  159.7 1.4 constant_dynamic-update-slice_fusion.33
  163.9 1.4 constant_dynamic-update-slice_fusion.30
  165.3 1.4 constant_dynamic-update-slice_fusion.29
  169.4 1.4 constant_dynamic-update-slice_fusion.26
  170.9 1.4 constant_dynamic-update-slice_fusion.25
  172.3 1.4 constant_dynamic-update-slice_fusion.24
  175.0 1.4 constant_dynamic-update-slice_fusion.22
  176.4 1.4 constant_dynamic-update-slice_fusion.21
  177.9 53.9 %all-gather.9.cloned.1.call-done = bf16[6144,384]{1,0:T(8,128)(2,1)} async-done(((bf16[96,384]{1,0:T(8,128)(2,1)}), bf16[6144,384]{1,0:T(8,128)(2,1)}) %all-gather.9.cloned.1.call-update) | async-done | bytes 4718608 | tf_op jit(solution)/shard_map/all_gather | solution.py:38
  231.8 4.3 fusion.10
  237.0 116.6 %all-gather.7.cloned.1.call-done = bf16[6144,384]{1,0:T(8,128)(2,1)} async-done(((bf16[96,384]{1,0:T(8,128)(2,1)}), bf16[6144,384]{1,0:T(8,128)(2,1)}) %all-gather.7.cloned.1.call-update) | async-done | bytes 4718608 | tf_op jit(solution)/shard_map/all_gather | solution.py:39
  353.6 4.0 fusion.7
  360.3 1.4 constant_dynamic-update-slice_fusion.18
  361.7 1.4 constant_dynamic-update-slice_fusion.17
  365.9 1.4 constant_dynamic-update-slice_fusion.14
  367.3 1.4 constant_dynamic-update-slice_fusion.13
  371.5 1.4 constant_dynamic-update-slice_fusion.10
  372.9 1.4 constant_dynamic-update-slice_fusion.9
  374.3 1.4 constant_dynamic-update-slice_fusion.8
  377.0 1.4 constant_dynamic-update-slice_fusion.6
  378.5 1.4 constant_dynamic-update-slice_fusion.5
  382.6 1.4 constant_dynamic-update-slice_fusion.2
  384.0 1.4 constant_dynamic-update-slice_fusion.1
  385.5 1.4 constant_dynamic-update-slice_fusion
  386.9 37.4 %all_to_all.5 = bf16[64,64,96]{2,1,0:T(8,128)(2,1)S(1)} all-to-all(bf16[64,64,96]{2,1,0:T(8,128)(2,1)} %constant_dynamic-update-slice_fusion), channel_id=1, replica_groups=mesh['fsdp'=64,'tp'=8] {'fsdp'}, dimensions={0} | all-to-all | bytes 1572864 | tf_op jit(solution)/shard_map/all_to_all | solution.py:49
  424.3 66.3 %all-gather.11.cloned.1.call-done = bf16[4096,384]{1,0:T(8,128)(2,1)} async-done(((bf16[64,384]{1,0:T(8,128)(2,1)}), bf16[4096,384]{1,0:T(8,128)(2,1)}) %all-gather.11.cloned.1.call-update) | async-done | bytes 3145744 | tf_op jit(solution)/shard_map/all_gather | solution.py:54
  490.6 3.3 fusion.11
  (49 shorter events, 42.0 us)
Async XLA Ops:
  7.2 101.9 %all-gather.5.cloned.1.call-start = ((), (), s32[]{:S(2)}) async-start(), calls=%async_computation.1 | async-start | bytes 3538944 | tf_op jit(solution)/shard_map/all_gather | solution.py:34
  7.9 223.9 %all-gather.9.cloned.1.call-start = ((), (), s32[]{:S(2)}) async-start(), calls=%async_computation.3 | async-start | bytes 4792320 | tf_op jit(solution)/shard_map/all_gather | solution.py:38
  9.8 343.8 %all-gather.7.cloned.1.call-start = ((), (), s32[]{:S(2)}) async-start(), calls=%async_computation.2 | async-start | bytes 4792320 | tf_op jit(solution)/shard_map/all_gather | solution.py:39
  10.5 480.1 %all-gather.11.cloned.1.call-start = ((), (), s32[]{:S(2)}) async-start(), calls=%async_computation.4 | async-start | bytes 3194880 | tf_op jit(solution)/shard_map/all_gather | solution.py:54
  109.1 2.8 copy-start
Sparse Core Ops, SparseCore 0:
  11.1 97.9 all-gather.4
  111.8 119.9 all-gather.8
  233.9 119.5 all-gather.6
  357.7 132.8 all-gather.10

commit v2 on v0

--- a/solution.py
+++ b/solution.py
@@ -35,7 +35,12 @@
     normed = layer_norm(whole)
     flat_all = normed.reshape(img_count * patch_count, D)
     picked = pick_rows(normed, keep_index).reshape(img_count * keep_count, D)
-    teacher_out = row_product(flat_all, lax.all_gather(teacher_panel, "fsdp", axis=0, tiled=True))
+    teacher_out = row_product(
+        flat_all,
+        jnp.concatenate(
+            lax.all_to_all(jnp.stack([teacher_panel] * lax.axis_size("fsdp")), "fsdp", 0, 0), axis=0
+        ),
+    )
     student_out = row_product(picked, lax.all_gather(student_panel, "fsdp", axis=0, tiled=True))
     teacher_out = teacher_out.reshape(img_count, patch_count, columns_dev)
     centre = jnp.mean(teacher_out, axis=1, keepdims=True)

time: 499 us -> 431 us (0.86); the launches traced: 499 us -> 426 us
  waiting for transfers between devices: 423 us -> 330 us
  starting transfers between devices: 0.16 us -> 15.8 us
    all_gather x1 -> x0, waiting for transfers between devices: 114 us -> none  [shards(): lax.all_gather(teacher_panel, 'fsdp', axis=0, tiled=True)]
    all_to_all x0 -> x1, waiting for transfers between devices: none -> 32.7 us  [shards(): lax.all_to_all(jnp.stack([teacher_panel] * lax.axis_size('fsdp')), 'fsdp'...]
    all_gather x1, waiting for transfers between devices: 116 us -> 94.7 us  [shards(): lax.all_gather(student_panel, 'fsdp', axis=0, tiled=True)]
    all_to_all x0 -> x1, starting transfers between devices: none -> 15.7 us  [shards(): lax.all_to_all(jnp.stack([teacher_panel] * lax.axis_size('fsdp')), 'fsdp'...]
    all_gather x1, waiting for transfers between devices: 97.9 us -> 109 us  [shards(): whole = lax.all_gather(images, 'tp', axis=2, tiled=True)]
  transfers between devices with their start and end apart: 4 -> 4, of which waited for: 4 -> 4; matrix products, arithmetic and copies ran while one was open for 3% -> 4% of each run, Pallas kernels for 0% -> 0%
where the time goes in v2:
time: 431 us; the launch traced here: 426 us
  waiting for transfers between devices  330 us (77%)
  blocking collectives  38.1 us (9%)
  starting transfers between devices  15.8 us (4%)
  between operations  13.8 us (3%)
  matrix products  11.6 us (3%)
  local copies, waits for them, and re-layouts  9.27 us (2%)
  other arithmetic  6.66 us (2%)
    all_gather x1, waiting for transfers between devices, shards(): whole = lax.all_gather(images, 'tp', axis=2, tiled=True)  109 us
    all_gather x1, waiting for transfers between devices, shards(): lax.all_gather(student_panel, 'fsdp', axis=0, tiled=True)  94.7 us
    all_gather x1, waiting for transfers between devices, shards(): lax.all_gather(error, 'fsdp', axis=0, tiled=True)  92.9 us
    all_to_all x1, blocking collectives, shards(): lax.all_to_all(picked, 'fsdp', split_axis=1, concat_axis=0, tiled=True)  38.1 us
    all_to_all x1, waiting for transfers between devices, shards(): lax.all_to_all(jnp.stack([teacher_panel] * lax.axis_size('fsdp')), 'fsdp'...  32.7 us
    all_to_all x1, starting transfers between devices, shards(): lax.all_to_all(jnp.stack([teacher_panel] * lax.axis_size('fsdp')), 'fsdp'...  15.7 us
  transfers between devices with their start and end apart: 4, of which 4 were waited for; matrix products, arithmetic and copies ran while one was open for 4% of the time, Pallas kernels for 0%

profile of v2, /device:TPU:1, one launch (start us, length us, event | category | flops | bytes accessed | tf_op | source)
XLA Modules:
  0.0 425.8 jit_solution(15391939949036122785)
XLA Ops:
  7.2 0.0 all-gather.4.cloned.1.call-start
  7.2 0.7 all-gather.4.cloned.1.call-update
  7.9 1.8 fusion.9
  9.7 2.7 stack.2
  12.3 0.0 copy-start.2
  12.3 15.7 %all-to-all-start.1 = ((bf16[64,96,384]{2,1,0:T(8,128)(2,1)}), bf16[64,96,384]{2,1,0:T(8,128)(2,1)}, u32[]{:S(2)}, u32[]{:S(2)}) async-start(bf16[64,96,384]{2,1,0:T(8,128)(2,1)} %stack.2), calls=%async_computation.1 | async-start | bytes 9437184 | tf_op jit(solution)/shard_map/all_to_all | solution.py:41
  28.0 0.0 all-gather.6.cloned.1.call-start
  28.1 0.7 all-gather.6.cloned.1.call-update
  28.8 0.0 all-gather.8.cloned.1.call-start
  28.8 0.0 copy-done.2
  28.9 108.8 %all-gather.4.cloned.1.call-done = bf16[1,256,6144]{2,1,0:T(8,128)(2,1)} async-done(((bf16[1,256,768]{2,1,0:T(8,128)(2,1)}), bf16[1,256,6144]{2,1,0:T(8,128)(2,1)}) %all-gather.4.cloned.1.call-update) | async-done | bytes 3145744 | tf_op jit(solution)/shard_map/all_gather | solution.py:34
  137.7 0.0 copy-start
  137.7 2.5 convert_reduce_fusion
  140.3 0.3 copy-done
  140.6 1.0 fusion.2
  141.5 1.2 fusion.3
  142.8 3.8 gather_fusion
  146.6 32.7 %all-to-all-done.1 = bf16[64,96,384]{2,1,0:T(8,128)(2,1)} async-done(((bf16[64,96,384]{2,1,0:T(8,128)(2,1)}), bf16[64,96,384]{2,1,0:T(8,128)(2,1)}, u32[]{:S(2)}, u32[]{:S(2)}) %all-to-all-start.1) | async-done | bytes 4718624 | tf_op jit(solution)/shard_map/all_to_all | solution.py:41
  179.3 4.3 %fusion.10 = (f32[384]{0:T(512)S(1)}, f32[256,384]{1,0:T(8,128)S(1)}) fusion(bf16[6144,384]{1,0:T(8,128)(2,1)} %bitcast.6, bf16[1,256,6144]{2,1,0:T(8,128)(2,1)S(1)} %fusion.3), kind=kOutput, calls=%fused_computation.25 | convolution fusion | flops 1208057472 | bytes 8259072 | tf_op jit(solution)/shard_map/dot_general | solution.py:23
  183.6 0.0 copy-start.1
  183.6 0.1 multiply_reduce_fusion
  183.7 0.8 gather_fusion.1
  184.5 94.7 %all-gather.6.cloned.1.call-done = bf16[6144,384]{1,0:T(8,128)(2,1)} async-done(((bf16[96,384]{1,0:T(8,128)(2,1)}), bf16[6144,384]{1,0:T(8,128)(2,1)}) %all-gather.6.cloned.1.call-update) | async-done | bytes 4718608 | tf_op jit(solution)/shard_map/all_gather | solution.py:44
  279.2 4.0 fusion.7
  283.2 0.0 all-gather.8.cloned.1.call-update
  283.2 0.0 copy-done.1
  283.2 1.0 all_to_all.17
  284.3 0.7 copy.6
  285.0 38.1 %all_to_all.24 = bf16[64,64,96]{2,0,1:T(8,128)(2,1)S(1)} all-to-all(bf16[64,64,96]{2,0,1:T(8,128)(2,1)S(1)} %copy.6), channel_id=1, replica_groups=mesh['fsdp'=64,'tp'=8] {'fsdp'}, dimensions={1} | all-to-all | bytes 1572864 | tf_op jit(solution)/shard_map/all_to_all | solution.py:53
  323.1 92.9 %all-gather.8.cloned.1.call-done = bf16[4096,384]{1,0:T(8,128)(2,1)} async-done(((bf16[64,384]{1,0:T(8,128)(2,1)}), bf16[4096,384]{1,0:T(8,128)(2,1)}) %all-gather.8.cloned.1.call-update) | async-done | bytes 3145744 | tf_op jit(solution)/shard_map/all_gather | solution.py:56
  416.0 3.2 fusion.11
  (8 shorter events, 0.1 us)
Async XLA Ops:
  7.2 130.6 %all-gather.4.cloned.1.call-start = ((), (), s32[]{:S(2)}) async-start(), calls=%async_computation.2 | async-start | bytes 3538944 | tf_op jit(solution)/shard_map/all_gather | solution.py:34
  12.3 16.5 %copy-start.2 = (s32[1,64]{1,0:T(1,128)S(1)}, s32[1,64]{1,0:T(1,128)}, u32[]{:S(2)}) copy-start(s32[1,64]{1,0:T(1,128)} %param.5) | copy-start | bytes 772
  12.3 166.9 %all-to-all-start.1 = ((bf16[64,96,384]{2,1,0:T(8,128)(2,1)}), bf16[64,96,384]{2,1,0:T(8,128)(2,1)}, u32[]{:S(2)}, u32[]{:S(2)}) async-start(bf16[64,96,384]{2,1,0:T(8,128)(2,1)} %stack.2), calls=%async_computation.1 | async-start | bytes 9437184 | tf_op jit(solution)/shard_map/all_to_all | solution.py:41
  28.0 251.2 %all-gather.6.cloned.1.call-start = ((), (), s32[]{:S(2)}) async-start(), calls=%async_computation.3 | async-start | bytes 4792320 | tf_op jit(solution)/shard_map/all_gather | solution.py:44
  28.8 387.2 %all-gather.8.cloned.1.call-start = ((), (), s32[]{:S(2)}) async-start(), calls=%async_computation.4 | async-start | bytes 3194880 | tf_op jit(solution)/shard_map/all_gather | solution.py:56
  137.7 2.8 copy-start
  183.6 99.7 %copy-start.1 = (bf16[64,6144]{1,0:T(8,128)(2,1)S(1)}, bf16[64,6144]{1,0:T(8,128)(2,1)}, u32[]{:S(2)}) copy-start(bf16[64,6144]{1,0:T(8,128)(2,1)} %gather_fusion) | copy-start | bytes 2359300
Sparse Core Ops, SparseCore 0:
  11.1 126.5 all-gather.3
  140.4 138.7 all-gather.5
  283.4 132.5 all-gather.7
